TPU v7x, 256 devices: a whole 4x4x8 slice. The times are simulated.
256 devices in a mesh: gx: 16 (over x, y), gy: 2 (over core), gz: 8 (over z).
Axes of the slice: x: 4, y: 4, z: 8, core: 2. Of those that a mesh axis runs over, the one named last changes fastest.
Arguments:
- field: float32 [2, 1024, 128, 1024], P(None, 'gx', 'gy', 'gz'), as said below
- start_basis: float32 [1024, 256], replicated, may hold values from -6 to 6
Outputs:
- factor: float32 [1024, 256], P('gx')
- core: float32 [2, 256, 128, 1024], P(None, 'gx', 'gy', 'gz')
Inputs may be any that keep to these rules, and one draw needn't show every extreme that they name: Real-valued field; no structure is promised.
All inputs are finite; a program needn't handle non-finite values.
Results may differ from a plain program's by a relative error of at most 0.0002.
Values sent between devices are 32-bit elements; how exact they have to be, the bound alone decides.
A program may use at most 64 MiB of HBM per device.

v0:
```python
import jax
import jax.numpy as jnp
from jax import lax
from jax.sharding import PartitionSpec as P

ITERS = 2


def orthonormal(image):
    small = jnp.dot(image.T, image, precision=lax.Precision.HIGHEST)
    lower = jnp.linalg.cholesky(small)
    return jax.scipy.linalg.solve_triangular(lower, image.T, lower=True).T


def per_device(field, start_basis):
    comps, slab, cells_y, cells_z = field.shape
    flat_field = field.reshape(comps, slab, cells_y * cells_z)
    fibers = lax.all_to_all(flat_field, "gx", split_axis=2, concat_axis=1, tiled=True)
    basis = start_basis
    local_gram = jnp.einsum("crm,csm->rs", fibers, fibers, precision=lax.Precision.HIGHEST)
    gram = lax.psum(local_gram, ("gx", "gy", "gz"))
    for step in range(ITERS):
        image = jnp.dot(gram, basis, precision=lax.Precision.HIGHEST)
        basis = orthonormal(image)
    projected = jnp.einsum("rk,crm->ckm", basis, fibers, precision=lax.Precision.HIGHEST)
    returned = lax.all_to_all(projected, "gx", split_axis=1, concat_axis=2, tiled=True)
    offset = lax.axis_index("gx") * slab
    factor = lax.dynamic_slice_in_dim(basis, offset, slab, 0)
    return (factor, returned.reshape(comps, returned.shape[1], cells_y, cells_z))


def solution(mesh):
    placed = (P(None, "gx", "gy", "gz"), P())
    return jax.shard_map(
        per_device,
        mesh=mesh,
        in_specs=placed,
        out_specs=(P("gx", None), P(None, "gx", "gy", "gz")),
        check_vma=False,
    )
```

profile of v0, /device:TPU:97, one launch (start us, length us, event | category | flops | bytes accessed | tf_op | source)
XLA Modules:
  0.0 604.0 jit_solution(12621777568615691695)
XLA Ops:
  7.2 0.0 copy-start
  7.2 0.0 all-reduce.3.cloned.1.call-start
  7.2 8.4 %copy.13 = f32[2,64,64,128]{1,0,3,2:T(2,128)} copy(f32[2,64,64,128]{3,2,1,0:T(8,128)} %param.5) | data formatting | bytes 8388608 | tf_op args[0]
  15.7 15.1 %reshape.52 = f32[16,1,65536]{2,1,0:T(1,128)} reshape(f32[8192,2,64]{2,1,0:T(2,128)} %bitcast.97) | data formatting | bytes 8388608
  30.8 56.1 %all_to_all.33 = f32[16,1,65536]{2,1,0:T(1,128)} all-to-all(f32[16,1,65536]{2,1,0:T(1,128)} %reshape.52), channel_id=1, replica_groups=mesh['gx'=16,'gy'=2,'gz'=8] {'gx'}, dimensions={0} | all-to-all | bytes 8388608 | tf_op jit(solution)/shard_map/all_to_all | solution.py:18
  86.8 0.5 broadcast.87
  87.3 13.7 %reduce.8 = f32[16,65536]{1,0:T(8,128)} reduce(f32[16,1,65536]{2,1,0:T(1,128)} %all_to_all.33, f32[]{:T(128)} %broadcast.87), dimensions={1}, to_apply=%all_to_all.24.reduce_sub_computation | reduce | bytes 8388612 | tf_op jit(solution)/shard_map/all_to_all | solution.py:18
  101.0 9.7 %reshape.53 = f32[8192,2,64]{2,1,0:T(2,128)} reshape(f32[16,65536]{1,0:T(8,128)} %reduce.8) | data formatting | bytes 8388608
  110.7 12.2 %copy.26 = f32[2,64,16,512]{3,1,2,0:T(8,128)} copy(f32[2,64,16,512]{1,0,3,2:T(2,128)} %bitcast.96) | data formatting | bytes 8388608 | tf_op jit(solution)/shard_map/all_to_all | solution.py:18
  122.9 17.6 %convolution_bitcast_fusion = f32[1024,1024]{1,0:T(8,128)} fusion(f32[2,1024,512]{2,1,0:T(8,128)} %bitcast.98), kind=kOutput, calls=%fused_computation.4 | convolution fusion | flops 12884901888 | bytes 8388608 | tf_op jit(solution)/shard_map/crm,csm->rs/dot_general | solution.py:20
  140.6 0.0 all-reduce.3.cloned.1.call-update
  140.6 270.4 %all-reduce.3.cloned.1.call-done = f32[1024,1024]{1,0:T(8,128)} async-done(((f32[1024,1024]{1,0:T(8,128)}), f32[1024,1024]{1,0:T(8,128)}) %all-reduce.3.cloned.1.call-update) | async-done | bytes 4194320 | tf_op jit(solution)/shard_map/psum | solution.py:21
  411.0 0.0 copy-done
  411.0 5.5 fusion.32
  416.5 1.8 fusion.33
  418.3 0.1 copy.16
  418.5 11.7 %cholesky.130 = f32[128,128]{1,0:T(8,128)S(1)} custom-call(f32[128,128]{1,0:T(8,128)S(1)} %cholesky.194), custom_call_target="Cholesky" | custom-call | tf_op jit(solution)/shard_map/jit(cholesky)/cholesky | solution.py:11
  430.3 9.8 %custom-call.13 = f32[1,128,128]{1,2,0:T(8,128)S(1)} custom-call(f32[1,128,128]{2,1,0:T(8,128)S(1)} %get-tuple-element.53), custom_call_target="InvertDiagBlocksLowerTriangular" | custom-call | tf_op jit(solution)/shard_map/jit(cholesky)/cholesky | solution.py:11
  440.1 0.2 constant_dynamic-update-slice_fusion.3
  440.3 0.3 convolution_subtract_fusion.3
  440.6 11.7 %cholesky.147 = f32[128,128]{1,0:T(8,128)S(1)} custom-call(f32[128,128]{1,0:T(8,128)S(1)} %convolution_subtract_fusion.3), custom_call_target="Cholesky" | custom-call | tf_op jit(solution)/shard_map/jit(cholesky)/cholesky | solution.py:11
  452.3 0.7 compare_reduce_fusion.2
  467.1 0.1 triangular_solve.75
  467.2 3.9 while.4
  467.2 0.6 fusion.55
  467.8 1.4 bitcast_dynamic-update-slice_fusion.4
  469.2 0.6 fusion.55
  469.8 1.4 bitcast_dynamic-update-slice_fusion.4
  471.2 19.7 %custom-call.14 = f32[2,128,128]{1,2,0:T(8,128)S(1)} custom-call(f32[2,128,128]{2,1,0:T(8,128)S(1)} %get-tuple-element.18), custom_call_target="InvertDiagBlocksLowerTriangular" | custom-call | tf_op jit(solution)/shard_map/jit(_solve_triangular)/triangular_solve | solution.py:12
  490.9 0.6 fusion.8
  491.5 1.0 convolution_subtract_fusion.1
  492.5 0.6 fusion.19
  493.2 5.3 fusion.2
  498.5 1.8 fusion.34
  500.3 0.1 copy.18
  500.5 11.7 %cholesky.164 = f32[128,128]{1,0:T(8,128)S(1)} custom-call(f32[128,128]{1,0:T(8,128)S(1)} %cholesky.197), custom_call_target="Cholesky" | custom-call | tf_op jit(solution)/shard_map/jit(cholesky)/cholesky | solution.py:11
  512.3 9.8 %custom-call.15 = f32[1,128,128]{1,2,0:T(8,128)S(1)} custom-call(f32[1,128,128]{2,1,0:T(8,128)S(1)} %get-tuple-element.49), custom_call_target="InvertDiagBlocksLowerTriangular" | custom-call | tf_op jit(solution)/shard_map/jit(cholesky)/cholesky | solution.py:11
  522.1 0.2 constant_dynamic-update-slice_fusion.1
  522.3 0.3 convolution_subtract_fusion.2
  522.6 11.7 %cholesky.181 = f32[128,128]{1,0:T(8,128)S(1)} custom-call(f32[128,128]{1,0:T(8,128)S(1)} %convolution_subtract_fusion.2), custom_call_target="Cholesky" | custom-call | tf_op jit(solution)/shard_map/jit(cholesky)/cholesky | solution.py:11
  534.3 0.6 compare_reduce_fusion
  535.0 0.6 compare_reduce_fusion.1
  536.9 0.2 select_select_fusion
  537.2 4.0 while.5
  537.2 0.6 fusion.56
  537.8 1.4 bitcast_dynamic-update-slice_fusion.5
  539.2 0.6 fusion.56
  539.8 1.4 bitcast_dynamic-update-slice_fusion.5
  541.2 19.7 %custom-call.16 = f32[2,128,128]{1,2,0:T(8,128)S(1)} custom-call(f32[2,128,128]{2,1,0:T(8,128)S(1)} %get-tuple-element.19), custom_call_target="InvertDiagBlocksLowerTriangular" | custom-call | tf_op jit(solution)/shard_map/jit(_solve_triangular)/triangular_solve | solution.py:12
  560.9 0.6 fusion.6
  561.5 1.0 convolution_subtract_fusion
  562.5 0.6 fusion.15
  563.2 5.7 convolution_bitcast_fusion.1
  568.9 1.8 copy.20
  570.7 4.6 all-to-all-start.1
  575.3 0.1 fusion.13
  575.4 0.7 copy.22
  576.1 17.8 %all-to-all-done.1 = f32[2,256,512]{2,0,1:T(2,128)} async-done(((f32[2,256,512]{2,0,1:T(2,128)}), f32[2,256,512]{2,0,1:T(2,128)}, u32[]{:S(2)}, u32[]{:S(2)}) %all-to-all-start.1) | async-done | bytes 1048608 | tf_op jit(solution)/shard_map/all_to_all | solution.py:26
  593.9 1.8 copy.21
  595.7 1.0 reshape.27
  (18 shorter events, 0.4 us)
Async XLA Ops:
  7.2 403.9 %copy-start = (f32[1024,256]{1,0:T(8,128)S(1)}, f32[1024,256]{1,0:T(8,128)}, u32[]{:S(2)}) copy-start(f32[1024,256]{1,0:T(8,128)} %param.6) | copy-start | bytes 3145732
  7.2 403.8 %all-reduce.3.cloned.1.call-start = ((), (), s32[]{:S(2)}) async-start(), calls=%async_computation.2 | async-start | bytes 8388608 | tf_op jit(solution)/shard_map/psum | solution.py:21
  570.7 23.2 %all-to-all-start.1 = ((f32[2,256,512]{2,0,1:T(2,128)}), f32[2,256,512]{2,0,1:T(2,128)}, u32[]{:S(2)}, u32[]{:S(2)}) async-start(f32[2,256,512]{2,0,1:T(2,128)} %copy.20), calls=%async_computation.1 | async-start | bytes 2097152 | tf_op jit(solution)/shard_map/all_to_all | solution.py:26
Sparse Core Ops, SparseCore 0:
  140.7 270.2 all-reduce.2
where the time goes:
time: 614 us; the launch traced here: 604 us
  waiting for transfers between devices  288 us (47%)
  other arithmetic  122 us (20%)
  local copies, waits for them, and re-layouts  59.5 us (10%)
  blocking collectives  56.1 us (9%)
  matrix products  43.3 us (7%)
  between operations  30.1 us (5%)
    psum x1, waiting for transfers between devices, per_device(): gram = lax.psum(local_gram, ('gx', 'gy', 'gz'))  270 us
    another operation x13, other arithmetic, orthonormal(): lower = jnp.linalg.cholesky(small)  68.5 us
    all_to_all x1, blocking collectives, per_device(): lax.all_to_all(flat_field, 'gx', split_axis=2, concat_axis=1, tiled=True)  56.1 us
    another operation x5, other arithmetic, orthonormal(): return jax.scipy.linalg.solve_triangular(lower, image.T, lower=True).T  39.6 us
    unnamed x6, local copies, waits for them, and re-layouts  33.9 us
    all_to_all x1, waiting for transfers between devices, per_device(): lax.all_to_all(projected, 'gx', split_axis=1, concat_axis=2, tiled=True)  17.8 us
    dot_general x1, matrix products, per_device(): jnp.einsum('crm,csm->rs', fibers, fibers, precision=lax.Precision.HIGHEST)  17.6 us
    all_to_all x1, other arithmetic, per_device(): lax.all_to_all(flat_field, 'gx', split_axis=2, concat_axis=1, tiled=True)  13.7 us
  transfers between devices with their start and end apart: 2, of which 2 were waited for; matrix products, arithmetic and copies ran while one was open for 0% of the time, Pallas kernels for 0%

commit v1 on v0

--- a/solution.py
+++ b/solution.py
@@ -4,6 +4,28 @@
 from jax.sharding import PartitionSpec as P
 
 ITERS = 2
+
+
+def cut_along(x, dim, size):
+    before, after = (x.shape[:dim], x.shape[dim + 1 :])
+    return jnp.moveaxis(x.reshape(*before, size, -1, *after), dim, 0)
+
+
+def joined_along(pieces, dim):
+    pieces = jnp.moveaxis(pieces, 0, dim)
+    dims = pieces.shape
+    return pieces.reshape(*dims[:dim], dims[dim] * dims[dim + 1], *dims[dim + 2 :])
+
+
+def pairwise_exchange(array, axis, split_dim, concat_dim):
+    count, index = (lax.axis_size(axis), lax.axis_index(axis))
+    parts = cut_along(array, split_dim, count)
+    gathered = [parts[index]]
+    for lap in range(1, count):
+        sent = parts[index ^ lap]
+        gathered.append(lax.ppermute(sent, axis, [(i, i ^ lap) for i in range(count)]))
+    parts = jnp.stack(gathered)[index ^ jnp.arange(count)]
+    return joined_along(parts, concat_dim)
 
 
 def orthonormal(image):
@@ -23,7 +45,7 @@
         image = jnp.dot(gram, basis, precision=lax.Precision.HIGHEST)
         basis = orthonormal(image)
     projected = jnp.einsum("rk,crm->ckm", basis, fibers, precision=lax.Precision.HIGHEST)
-    returned = lax.all_to_all(projected, "gx", split_axis=1, concat_axis=2, tiled=True)
+    returned = pairwise_exchange(projected, "gx", 1, 2)
     offset = lax.axis_index("gx") * slab
     factor = lax.dynamic_slice_in_dim(basis, offset, slab, 0)
     return (factor, returned.reshape(comps, returned.shape[1], cells_y, cells_z))

time: 614 us -> 633 us (1.031)
  the two profiles are of different devices: /device:TPU:97 before, /device:TPU:6 now
where the time goes in v1:
time: 633 us; the launch traced here: 622 us
  waiting for transfers between devices  275 us (43%)
  other arithmetic  122 us (19%)
  local copies, waits for them, and re-layouts  62.4 us (10%)
  blocking collectives  56.9 us (9%)
  matrix products  43.3 us (7%)
  starting transfers between devices  32.4 us (5%)
  between operations  30.4 us (5%)
    psum x1, waiting for transfers between devices, per_device(): gram = lax.psum(local_gram, ('gx', 'gy', 'gz'))  270 us
    another operation x13, other arithmetic, orthonormal(): lower = jnp.linalg.cholesky(small)  68.6 us
    all_to_all x1, blocking collectives, per_device(): lax.all_to_all(flat_field, 'gx', split_axis=2, concat_axis=1, tiled=True)  56.9 us
    another operation x5, other arithmetic, orthonormal(): return jax.scipy.linalg.solve_triangular(lower, image.T, lower=True).T  39.6 us
    unnamed x21, local copies, waits for them, and re-layouts  38.2 us
    ppermute x15, starting transfers between devices, pairwise_exchange(): lax.ppermute(sent, axis, [(i, i ^ lap) for i in range(count)])  32.4 us
    dot_general x1, matrix products, per_device(): jnp.einsum('crm,csm->rs', fibers, fibers, precision=lax.Precision.HIGHEST)  17.6 us
    all_to_all x1, other arithmetic, per_device(): lax.all_to_all(flat_field, 'gx', split_axis=2, concat_axis=1, tiled=True)  13.7 us
  transfers between devices with their start and end apart: 16, of which 2 were waited for; matrix products, arithmetic and copies ran while one was open for 1% of the time, Pallas kernels for 0%

profile of v1, /device:TPU:6, one launch (start us, length us, event | category | flops | bytes accessed | tf_op | source)
XLA Modules:
  0.0 622.3 jit_solution(9169383479604928725)
XLA Ops:
  7.2 8.4 %copy.18 = f32[2,64,64,128]{1,0,3,2:T(2,128)} copy(f32[2,64,64,128]{3,2,1,0:T(8,128)} %param.5) | data formatting | bytes 8388608 | tf_op args[0]
  15.7 15.1 %reshape.106 = f32[16,1,65536]{2,1,0:T(1,128)} reshape(f32[8192,2,64]{2,1,0:T(2,128)} %bitcast.160) | data formatting | bytes 8388608
  30.8 56.9 %all_to_all.18 = f32[16,1,65536]{2,1,0:T(1,128)} all-to-all(f32[16,1,65536]{2,1,0:T(1,128)} %reshape.106), channel_id=1, replica_groups=mesh['gx'=16,'gy'=2,'gz'=8] {'gx'}, dimensions={0} | all-to-all | bytes 8388608 | tf_op jit(solution)/shard_map/all_to_all | solution.py:40
  88.2 13.7 %reduce.8 = f32[16,65536]{1,0:T(8,128)} reduce(f32[16,1,65536]{2,1,0:T(1,128)} %all_to_all.18, f32[]{:T(128)} %broadcast.122), dimensions={1}, to_apply=%all_to_all.13.reduce_sub_computation | reduce | bytes 8388612 | tf_op jit(solution)/shard_map/all_to_all | solution.py:40
  101.9 9.7 %reshape.107 = f32[8192,2,64]{2,1,0:T(2,128)} reshape(f32[16,65536]{1,0:T(8,128)} %reduce.8) | data formatting | bytes 8388608
  111.5 12.2 %copy.30 = f32[2,64,16,512]{3,1,2,0:T(8,128)} copy(f32[2,64,16,512]{1,0,3,2:T(2,128)} %bitcast.159) | data formatting | bytes 8388608 | tf_op jit(solution)/shard_map/all_to_all | solution.py:40
  123.7 17.6 %convolution_bitcast_fusion = f32[1024,1024]{1,0:T(8,128)} fusion(f32[2,1024,512]{2,1,0:T(8,128)} %bitcast.161), kind=kOutput, calls=%fused_computation.5 | convolution fusion | flops 12884901888 | bytes 8388608 | tf_op jit(solution)/shard_map/crm,csm->rs/dot_general | solution.py:42
  141.5 269.7 %all-reduce.3.cloned.1.call-done = f32[1024,1024]{1,0:T(8,128)} async-done(((f32[1024,1024]{1,0:T(8,128)}), f32[1024,1024]{1,0:T(8,128)}) %all-reduce.3.cloned.1.call-update) | async-done | bytes 4194320 | tf_op jit(solution)/shard_map/psum | solution.py:43
  411.3 5.5 fusion.34
  416.7 1.8 fusion.35
  418.8 11.7 %cholesky.130 = f32[128,128]{1,0:T(8,128)S(1)} custom-call(f32[128,128]{1,0:T(8,128)S(1)} %cholesky.194), custom_call_target="Cholesky" | custom-call | tf_op jit(solution)/shard_map/jit(cholesky)/cholesky | solution.py:33
  430.5 9.8 %custom-call.13 = f32[1,128,128]{1,2,0:T(8,128)S(1)} custom-call(f32[1,128,128]{2,1,0:T(8,128)S(1)} %get-tuple-element.70), custom_call_target="InvertDiagBlocksLowerTriangular" | custom-call | tf_op jit(solution)/shard_map/jit(cholesky)/cholesky | solution.py:33
  440.8 11.7 %cholesky.147 = f32[128,128]{1,0:T(8,128)S(1)} custom-call(f32[128,128]{1,0:T(8,128)S(1)} %convolution_subtract_fusion.3), custom_call_target="Cholesky" | custom-call | tf_op jit(solution)/shard_map/jit(cholesky)/cholesky | solution.py:33
  452.6 0.7 compare_reduce_fusion.2
  467.6 4.1 while.4
  467.6 0.6 fusion.57
  468.2 1.4 bitcast_dynamic-update-slice_fusion.20
  469.7 0.6 fusion.57
  470.3 1.4 bitcast_dynamic-update-slice_fusion.20
  471.7 19.7 %custom-call.14 = f32[2,128,128]{1,2,0:T(8,128)S(1)} custom-call(f32[2,128,128]{2,1,0:T(8,128)S(1)} %get-tuple-element.18), custom_call_target="InvertDiagBlocksLowerTriangular" | custom-call | tf_op jit(solution)/shard_map/jit(_solve_triangular)/triangular_solve | solution.py:34
  491.4 0.6 fusion.9
  492.1 1.0 convolution_subtract_fusion.1
  493.1 0.6 fusion.20
  493.7 5.3 fusion.3
  499.0 1.8 fusion.36
  501.1 11.7 %cholesky.164 = f32[128,128]{1,0:T(8,128)S(1)} custom-call(f32[128,128]{1,0:T(8,128)S(1)} %cholesky.197), custom_call_target="Cholesky" | custom-call | tf_op jit(solution)/shard_map/jit(cholesky)/cholesky | solution.py:33
  512.9 9.8 %custom-call.15 = f32[1,128,128]{1,2,0:T(8,128)S(1)} custom-call(f32[1,128,128]{2,1,0:T(8,128)S(1)} %get-tuple-element.66), custom_call_target="InvertDiagBlocksLowerTriangular" | custom-call | tf_op jit(solution)/shard_map/jit(cholesky)/cholesky | solution.py:33
  523.2 11.7 %cholesky.181 = f32[128,128]{1,0:T(8,128)S(1)} custom-call(f32[128,128]{1,0:T(8,128)S(1)} %convolution_subtract_fusion.2), custom_call_target="Cholesky" | custom-call | tf_op jit(solution)/shard_map/jit(cholesky)/cholesky | solution.py:33
  534.9 0.6 compare_reduce_fusion
  535.5 0.6 compare_reduce_fusion.1
  537.7 4.0 while.5
  537.8 0.6 fusion.58
  538.4 1.4 bitcast_dynamic-update-slice_fusion.21
  539.8 0.6 fusion.58
  540.4 1.4 bitcast_dynamic-update-slice_fusion.21
  541.8 19.7 %custom-call.16 = f32[2,128,128]{1,2,0:T(8,128)S(1)} custom-call(f32[2,128,128]{2,1,0:T(8,128)S(1)} %get-tuple-element.19), custom_call_target="InvertDiagBlocksLowerTriangular" | custom-call | tf_op jit(solution)/shard_map/jit(_solve_triangular)/triangular_solve | solution.py:34
  561.4 0.6 fusion.7
  562.1 1.0 convolution_subtract_fusion
  563.1 0.6 fusion.16
  563.7 5.7 fusion.1
  569.5 0.8 dynamic-slice_bitcast_fusion
  570.3 1.1 collective-permute-start
  571.5 1.8 collective-permute-start.1
  573.3 1.7 collective-permute-start.2
  575.0 0.9 collective-permute-start.3
  575.9 0.5 collective-permute-start.4
  576.5 0.7 copy.26
  577.3 4.2 collective-permute-start.5
  581.5 0.8 bitcast_dynamic-update-slice_fusion.16
  582.3 1.6 collective-permute-start.6
  583.9 0.8 bitcast_dynamic-update-slice_fusion.15
  584.8 1.5 collective-permute-start.7
  586.3 0.8 bitcast_dynamic-update-slice_fusion.14
  587.5 0.8 bitcast_dynamic-update-slice_fusion.13
  588.3 6.4 %collective-permute-start.9 = (f32[2,16,512]{2,1,0:T(8,128)S(1)}, f32[2,16,512]{2,1,0:T(8,128)S(1)}, u32[]{:S(2)}, u32[]{:S(2)}) collective-permute-start(f32[2,16,512]{2,1,0:T(8,128)S(1)} %get-tuple-element.53), channel_id=1, source_target_pairs={{0,160},{16,176},{32,128},{48,144},{64,224},{80,240},{96,192},{112... | collective-permute-start | bytes 196616 | tf_op jit(solution)/shard_map/ppermute | solution.py:26
  594.7 0.8 bitcast_dynamic-update-slice_fusion.12
  595.6 2.4 collective-permute-start.10
  598.0 0.5 collective-permute-start.11
  598.7 6.4 %collective-permute-start.13 = (f32[2,16,512]{2,1,0:T(8,128)S(1)}, f32[2,16,512]{2,1,0:T(8,128)S(1)}, u32[]{:S(2)}, u32[]{:S(2)}) collective-permute-start(f32[2,16,512]{2,1,0:T(8,128)S(1)} %get-tuple-element.49), channel_id=1, source_target_pairs={{0,224},{16,240},{32,192},{48,208},{64,160},{80,176},{96,128},{112... | collective-permute-start | bytes 196616 | tf_op jit(solution)/shard_map/ppermute | solution.py:26
  605.1 2.8 collective-permute-start.14
  608.0 4.8 collective-permute-done.14
  612.7 0.6 gather_fusion
  613.4 0.6 copy.25
  614.0 1.0 reshape_reshape.3
  (61 shorter events, 3.1 us)
Async XLA Ops:
  7.2 404.1 %copy-start = (f32[1024,256]{1,0:T(8,128)S(1)}, f32[1024,256]{1,0:T(8,128)}, u32[]{:S(2)}) copy-start(f32[1024,256]{1,0:T(8,128)} %param.6) | copy-start | bytes 3145732
  7.2 404.1 %all-reduce.3.cloned.1.call-start = ((), (), s32[]{:S(2)}) async-start(), calls=%async_computation.1 | async-start | bytes 8388608 | tf_op jit(solution)/shard_map/psum | solution.py:43
  570.3 6.9 %collective-permute-start = (f32[2,16,512]{2,1,0:T(8,128)}, f32[2,16,512]{2,1,0:T(8,128)}, u32[]{:S(2)}, u32[]{:S(2)}) collective-permute-start(f32[2,16,512]{2,1,0:T(8,128)} %get-tuple-element.62), channel_id=1, source_target_pairs={{0,16},{16,0},{32,48},{48,32},{64,80},{80,64},{96,112},{112,96},{1... | collective-permute-start | bytes 196616 | tf_op jit(solution)/shard_map/ppermute | solution.py:26
  571.5 10.9 %collective-permute-start.1 = (f32[2,16,512]{2,1,0:T(8,128)}, f32[2,16,512]{2,1,0:T(8,128)}, u32[]{:S(2)}, u32[]{:S(2)}) collective-permute-start(f32[2,16,512]{2,1,0:T(8,128)} %get-tuple-element.61), channel_id=1, source_target_pairs={{0,32},{16,48},{32,0},{48,16},{64,96},{80,112},{96,64},{112,80},{1... | collective-permute-start | bytes 196616 | tf_op jit(solution)/shard_map/ppermute | solution.py:26
  573.3 11.5 %collective-permute-start.2 = (f32[2,16,512]{2,1,0:T(8,128)}, f32[2,16,512]{2,1,0:T(8,128)}, u32[]{:S(2)}, u32[]{:S(2)}) collective-permute-start(f32[2,16,512]{2,1,0:T(8,128)} %get-tuple-element.60), channel_id=1, source_target_pairs={{0,48},{16,32},{32,16},{48,0},{64,112},{80,96},{96,80},{112,64},{1... | collective-permute-start | bytes 196616 | tf_op jit(solution)/shard_map/ppermute | solution.py:26
  575.0 12.1 %collective-permute-start.3 = (f32[2,16,512]{2,1,0:T(8,128)}, f32[2,16,512]{2,1,0:T(8,128)}, u32[]{:S(2)}, u32[]{:S(2)}) collective-permute-start(f32[2,16,512]{2,1,0:T(8,128)} %get-tuple-element.59), channel_id=1, source_target_pairs={{0,64},{16,80},{32,96},{48,112},{64,0},{80,16},{96,32},{112,48},{1... | collective-permute-start | bytes 196616 | tf_op jit(solution)/shard_map/ppermute | solution.py:26
  575.9 12.5 %collective-permute-start.4 = (f32[2,16,512]{2,1,0:T(8,128)}, f32[2,16,512]{2,1,0:T(8,128)}, u32[]{:S(2)}, u32[]{:S(2)}) collective-permute-start(f32[2,16,512]{2,1,0:T(8,128)} %get-tuple-element.58), channel_id=1, source_target_pairs={{0,80},{16,64},{32,112},{48,96},{64,16},{80,0},{96,48},{112,32},{1... | collective-permute-start | bytes 196616 | tf_op jit(solution)/shard_map/ppermute | solution.py:26
  577.3 18.3 %collective-permute-start.5 = (f32[2,16,512]{2,1,0:T(8,128)}, f32[2,16,512]{2,1,0:T(8,128)S(1)}, u32[]{:S(2)}, u32[]{:S(2)}) collective-permute-start(f32[2,16,512]{2,1,0:T(8,128)} %get-tuple-element.57), channel_id=1, source_target_pairs={{0,96},{16,112},{32,64},{48,80},{64,32},{80,48},{96,0},{112,16},{1... | collective-permute-start | bytes 196616 | tf_op jit(solution)/shard_map/ppermute | solution.py:26
  582.3 15.7 %collective-permute-start.6 = (f32[2,16,512]{2,1,0:T(8,128)}, f32[2,16,512]{2,1,0:T(8,128)S(1)}, u32[]{:S(2)}, u32[]{:S(2)}) collective-permute-start(f32[2,16,512]{2,1,0:T(8,128)} %get-tuple-element.56), channel_id=1, source_target_pairs={{0,112},{16,96},{32,80},{48,64},{64,48},{80,32},{96,16},{112,0},{1... | collective-permute-start | bytes 196616 | tf_op jit(solution)/shard_map/ppermute | solution.py:26
  584.8 13.7 %collective-permute-start.7 = (f32[2,16,512]{2,1,0:T(8,128)}, f32[2,16,512]{2,1,0:T(8,128)S(1)}, u32[]{:S(2)}, u32[]{:S(2)}) collective-permute-start(f32[2,16,512]{2,1,0:T(8,128)} %get-tuple-element.55), channel_id=1, source_target_pairs={{0,128},{16,144},{32,160},{48,176},{64,192},{80,208},{96,224},{112... | collective-permute-start | bytes 196616 | tf_op jit(solution)/shard_map/ppermute | solution.py:26
  587.2 11.5 %collective-permute-start.8 = (f32[2,16,512]{2,1,0:T(8,128)}, f32[2,16,512]{2,1,0:T(8,128)S(1)}, u32[]{:S(2)}, u32[]{:S(2)}) collective-permute-start(f32[2,16,512]{2,1,0:T(8,128)} %get-tuple-element.54), channel_id=1, source_target_pairs={{0,144},{16,128},{32,176},{48,160},{64,208},{80,192},{96,240},{112... | collective-permute-start | bytes 196616 | tf_op jit(solution)/shard_map/ppermute | solution.py:26
  588.3 16.7 %collective-permute-start.9 = (f32[2,16,512]{2,1,0:T(8,128)S(1)}, f32[2,16,512]{2,1,0:T(8,128)S(1)}, u32[]{:S(2)}, u32[]{:S(2)}) collective-permute-start(f32[2,16,512]{2,1,0:T(8,128)S(1)} %get-tuple-element.53), channel_id=1, source_target_pairs={{0,160},{16,176},{32,128},{48,144},{64,224},{80,240},{96,192},{112... | collective-permute-start | bytes 196616 | tf_op jit(solution)/shard_map/ppermute | solution.py:26
  595.6 12.3 %collective-permute-start.10 = (f32[2,16,512]{2,1,0:T(8,128)S(1)}, f32[2,16,512]{2,1,0:T(8,128)S(1)}, u32[]{:S(2)}, u32[]{:S(2)}) collective-permute-start(f32[2,16,512]{2,1,0:T(8,128)S(1)} %get-tuple-element.52), channel_id=1, source_target_pairs={{0,176},{16,160},{32,144},{48,128},{64,240},{80,224},{96,208},{112... | collective-permute-start | bytes 196616 | tf_op jit(solution)/shard_map/ppermute | solution.py:26
  598.0 9.9 %collective-permute-start.11 = (f32[2,16,512]{2,1,0:T(8,128)S(1)}, f32[2,16,512]{2,1,0:T(8,128)S(1)}, u32[]{:S(2)}, u32[]{:S(2)}) collective-permute-start(f32[2,16,512]{2,1,0:T(8,128)S(1)} %get-tuple-element.51), channel_id=1, source_target_pairs={{0,192},{16,208},{32,224},{48,240},{64,128},{80,144},{96,160},{112... | collective-permute-start | bytes 196616 | tf_op jit(solution)/shard_map/ppermute | solution.py:26
  598.5 9.4 %collective-permute-start.12 = (f32[2,16,512]{2,1,0:T(8,128)S(1)}, f32[2,16,512]{2,1,0:T(8,128)S(1)}, u32[]{:S(2)}, u32[]{:S(2)}) collective-permute-start(f32[2,16,512]{2,1,0:T(8,128)S(1)} %get-tuple-element.50), channel_id=1, source_target_pairs={{0,208},{16,192},{32,240},{48,224},{64,144},{80,128},{96,176},{112... | collective-permute-start | bytes 196616 | tf_op jit(solution)/shard_map/ppermute | solution.py:26
  598.7 9.3 %collective-permute-start.13 = (f32[2,16,512]{2,1,0:T(8,128)S(1)}, f32[2,16,512]{2,1,0:T(8,128)S(1)}, u32[]{:S(2)}, u32[]{:S(2)}) collective-permute-start(f32[2,16,512]{2,1,0:T(8,128)S(1)} %get-tuple-element.49), channel_id=1, source_target_pairs={{0,224},{16,240},{32,192},{48,208},{64,160},{80,176},{96,128},{112... | collective-permute-start | bytes 196616 | tf_op jit(solution)/shard_map/ppermute | solution.py:26
  605.1 7.7 %collective-permute-start.14 = (f32[2,16,512]{2,1,0:T(8,128)S(1)}, f32[2,16,512]{2,1,0:T(8,128)S(1)}, u32[]{:S(2)}, u32[]{:S(2)}) collective-permute-start(f32[2,16,512]{2,1,0:T(8,128)S(1)} %get-tuple-element.48), channel_id=1, source_target_pairs={{0,240},{16,224},{32,208},{48,192},{64,176},{80,160},{96,144},{112... | collective-permute-start | bytes 196616 | tf_op jit(solution)/shard_map/ppermute | solution.py:26
Sparse Core Ops, SparseCore 0:
  141.5 269.6 all-reduce.2
